TPU v7x, 32 devices: a whole 2x2x4 slice. The times are simulated.
32 devices in a mesh: person: 4 (over z), variant: 8 (over y, x, core).
Axes of the slice: x: 2, y: 2, z: 4, core: 2. Of those that a mesh axis runs over, the one named last changes fastest.
Arguments:
- dosages: bfloat16 [20480, 8192], P('person', 'variant'), may hold values from -6 to 6
- phenotypes: bfloat16 [20480, 128], P(('person', 'variant')), may hold values from -16 to 16
- coefficients: float32 [8192, 128], P('variant'), may hold values from -5 to 5
- trait_precision: float32 [128], replicated, may hold values from 1 to 4
- noise: bfloat16 [8192, 128], P('variant'), may hold values from -6 to 6
- band_diag: bfloat16 [8192, 512], P('variant'), may hold values from -2 to 2
- band_lower: bfloat16 [8192, 512], P('variant'), may hold values from -0.125 to 0.125
Outputs:
- proposal: float32 [8192, 128], P('variant')
- residual: float32 [20480, 128], P(('person', 'variant'))
All inputs are finite; a program needn't handle non-finite values.
Results may differ from a plain program's by a relative error of at most 0.02.
Values may be sent and summed in bfloat16 or wider, within the bound.
A program may use at most 64 MiB of HBM per device.

v0:
```python
import math

import jax
import jax.numpy as jnp
from jax import lax
from jax.sharding import PartitionSpec as P

step_size = 0.25


def shifted(block, axis, distance):
    devices = range(lax.axis_size(axis))
    route = [(i - distance, i) for i in devices if i - distance in devices]
    return lax.ppermute(block, axis, route)


def precondition(gradient, coef_part, noise_part, band_diag, band_lower):
    variants, columns = gradient.shape
    band_width = band_diag.shape[1]
    blocks = variants // band_width
    diag_blocks = band_diag.reshape(blocks, band_width, band_width)
    lower_blocks = band_lower.reshape(blocks, band_width, band_width)
    grad_blocks = gradient.astype(jnp.bfloat16).reshape(blocks, band_width, columns)
    own_term = jnp.einsum(
        "bij,bik->bjk", diag_blocks, grad_blocks, preferred_element_type=jnp.float32
    )
    upward = jnp.einsum(
        "bij,bik->bjk", lower_blocks, grad_blocks, preferred_element_type=jnp.float32
    )
    incoming = shifted(upward[0].astype(jnp.bfloat16), "variant", -1).astype(jnp.float32)
    pulled = own_term + jnp.concatenate([upward[1:], incoming[None]], 0)
    update = step_size / 2.0 * pulled + math.sqrt(step_size) * noise_part.astype(
        jnp.float32
    ).reshape(blocks, band_width, columns)
    update_half = update.astype(jnp.bfloat16)
    carried = shifted(update_half[-1], "variant", 1)
    previous = jnp.concatenate([carried[None], update_half[:-1]], 0)
    result = coef_part.reshape(blocks, band_width, columns)
    result = result + jnp.einsum(
        "bij,bjk->bik", diag_blocks, update_half, preferred_element_type=jnp.float32
    )
    result = result + jnp.einsum(
        "bij,bjk->bik", lower_blocks, previous, preferred_element_type=jnp.float32
    )
    return result.reshape(variants, columns)


def local(dosages, phenotypes, coefficients, trait_precision, noise, band_diag, band_lower):
    people, variants = dosages.shape
    inverse_root = 1.0 / math.sqrt(variants * lax.axis_size("variant"))
    coef_half = coefficients.astype(jnp.bfloat16)
    contract_rows = (((0,), (0,)), ((), ()))
    row_block = dosages
    pred_piece = lax.psum_scatter(
        jnp.dot(row_block, coef_half, preferred_element_type=jnp.float32).astype(jnp.bfloat16),
        "variant",
        scatter_dimension=0,
        tiled=True,
    ).astype(jnp.float32)
    residual = phenotypes.astype(jnp.float32) - pred_piece * inverse_root
    row_block = dosages
    grad_part = lax.dot_general(
        row_block,
        lax.all_gather(residual.astype(jnp.bfloat16), "variant", axis=0, tiled=True),
        contract_rows,
        preferred_element_type=jnp.float32,
    )
    summed = lax.psum(grad_part.astype(jnp.bfloat16), "person").astype(jnp.float32)
    gradient = summed * inverse_root * trait_precision[None, :] - coefficients
    proposal = precondition(gradient, coefficients, noise, band_diag, band_lower)
    return (proposal, residual)


def solution(mesh):
    placed = (
        P("person", "variant"),
        P(("person", "variant"), None),
        P("variant", None),
        P(),
        P("variant", None),
        P("variant", None),
        P("variant", None),
    )
    return jax.shard_map(
        local,
        mesh=mesh,
        in_specs=placed,
        out_specs=(P("variant", None), P(("person", "variant"), None)),
        check_vma=False,
    )
```

profile of v0, /device:TPU:4, one launch (start us, length us, event | category | flops | bytes accessed | tf_op | source)
XLA Modules:
  0.0 147.9 jit_solution(18286986551421334629)
XLA Ops:
  7.2 0.0 reduce-scatter.2.cloned.1.call-start
  7.2 8.1 %convolution_convert_fusion = bf16[5120,128]{1,0:T(8,128)(2,1)} fusion(bf16[5120,1024]{1,0:T(8,128)(2,1)} %param.7, f32[1024,128]{1,0:T(8,128)} %param.9), kind=kOutput, calls=%fused_computation | convolution fusion | flops 1342963712 | bytes 12320768 | tf_op jit(solution)/shard_map/dot_general | solution.py:55
  15.4 0.0 all-gather.2.cloned.1.call-start
  15.4 38.4 %reduce-scatter.2.cloned.1.call-done = bf16[640,128]{1,0:T(8,128)(2,1)} async-done(((bf16[5120,128]{1,0:T(8,128)(2,1)}), bf16[640,128]{1,0:T(8,128)(2,1)}) %reduce-scatter.2.cloned.1.call-update) | async-done | bytes 163856 | tf_op jit(solution)/shard_map/reduce_scatter | solution.py:54
  53.9 1.7 %fusion.18 = (bf16[640,128]{1,0:T(8,128)(2,1)}, f32[640,128]{1,0:T(8,128)}) fusion(bf16[640,128]{1,0:T(8,128)(2,1)} %reduce-scatter.2.cloned.1.call-done, bf16[640,128]{1,0:T(8,128)(2,1)S(1)} %copy-done.4), kind=kLoop, calls=%fused_computation.30 | loop fusion | flops 409600 | bytes 819200 | tf_op jit(solution)/shard_map/convert_element_type | solution.py:64
  55.7 0.0 all-reduce.2.cloned.1.call-start
  55.7 25.1 %all-gather.2.cloned.1.call-done = bf16[5120,128]{1,0:T(8,128)(2,1)} async-done(((bf16[640,128]{1,0:T(8,128)(2,1)}), bf16[5120,128]{1,0:T(8,128)(2,1)}) %all-gather.2.cloned.1.call-update) | async-done | bytes 1310736 | tf_op jit(solution)/shard_map/all_gather | solution.py:64
  80.8 6.6 %fusion.2 = bf16[1024,128]{0,1:T(8,128)(2,1)} fusion(bf16[5120,128]{1,0:T(8,128)(2,1)} %all-gather.2.cloned.1.call-done, bf16[5120,1024]{1,0:T(8,128)(2,1)} %param.7), kind=kOutput, calls=%fused_computation.8 | convolution fusion | flops 1342308352 | bytes 12058624 | tf_op jit(solution)/shard_map/dot_general | solution.py:62
  87.5 0.2 copy.12
  87.7 35.5 %all-reduce.2.cloned.1.call-done = bf16[1024,128]{0,1:T(8,128)(2,1)} async-done(((bf16[1024,128]{0,1:T(8,128)(2,1)}), bf16[1024,128]{0,1:T(8,128)(2,1)}) %all-reduce.2.cloned.1.call-update) | async-done | bytes 262160 | tf_op jit(solution)/shard_map/psum | solution.py:68
  123.3 1.1 subtract_convert_fusion
  124.4 0.3 convolution_bitcast_fusion.2
  124.7 0.7 fusion.16
  125.4 1.9 %collective-permute-start = (bf16[512,128]{0,1:T(8,128)(2,1)}, bf16[512,128]{0,1:T(8,128)(2,1)S(1)}, u32[]{:S(2)}, u32[]{:S(2)}) collective-permute-start(bf16[512,128]{0,1:T(8,128)(2,1)} %fusion.16), channel_id=1, source_target_pairs={{1,0},{2,1},{3,2},{4,3},{5,4},{6,5},{7,6},{9,8},{10,9},{11,10},{12... | collective-permute-start | bytes 393224 | tf_op jit(solution)/shard_map/ppermute | solution.py:14
  127.3 1.8 %convert_multiply_fusion = f32[1024,128]{1,0:T(8,128)} fusion(bf16[1024,128]{1,0:T(8,128)(2,1)} %param.11), kind=kLoop, calls=%fused_computation.13 | loop fusion | flops 262144 | bytes 786432 | tf_op jit(solution)/shard_map/mul | solution.py:32
  129.1 1.2 copy.15
  130.3 1.0 copy.16
  131.3 1.0 slice.17
  132.3 0.3 fusion.5
  132.7 2.4 %collective-permute-start.1 = (bf16[512,128]{0,1:T(8,128)(2,1)S(1)}, bf16[512,128]{0,1:T(8,128)(2,1)S(1)}, u32[]{:S(2)}, u32[]{:S(2)}) collective-permute-start(bf16[512,128]{0,1:T(8,128)(2,1)S(1)} %get-tuple-element.4), channel_id=1, source_target_pairs={{0,1},{1,2},{2,3},{3,4},{4,5},{5,6},{6,7},{8,9},{9,10},{10,11},{11... | collective-permute-start | bytes 393224 | tf_op jit(solution)/shard_map/ppermute | solution.py:14
  135.1 1.5 %fusion.1 = f32[2,512,128]{1,2,0:T(8,128)S(1)} fusion(f32[2,512,128]{1,2,0:T(8,128)} %copy.16, bf16[2,512,128]{1,2,0:T(8,128)(2,1)S(1)} %fusion.5, bf16[2,512,512]{2,1,0:T(8,128)(2,1)S(1)} %bitcast.46), kind=kOutput, calls=%fused_computation.4 | convolution fusion | flops 134348800 | bytes 2359296 | tf_op jit(solution)/shard_map/bij,bjk->bik/dot_general | solution.py:39
  136.6 3.2 %collective-permute-done.1 = bf16[512,128]{0,1:T(8,128)(2,1)S(1)} collective-permute-done((bf16[512,128]{0,1:T(8,128)(2,1)S(1)}, bf16[512,128]{0,1:T(8,128)(2,1)S(1)}, u32[]{:S(2)}, u32[]{:S(2)}) %collective-permute-start.1) | collective-permute-done | bytes 131104 | tf_op jit(solution)/shard_map/ppermute | solution.py:14
  139.9 0.5 fusion
  140.4 1.0 copy.17
  (19 shorter events, 0.1 us)
Async XLA Ops:
  7.2 125.2 %copy-start = (bf16[1024,512]{1,0:T(8,128)(2,1)S(1)}, bf16[1024,512]{1,0:T(8,128)(2,1)}, u32[]{:S(2)}) copy-start(bf16[1024,512]{1,0:T(8,128)(2,1)} %param.12) | copy-start | bytes 3145732
  7.2 46.7 %copy-start.4 = (bf16[640,128]{1,0:T(8,128)(2,1)S(1)}, bf16[640,128]{1,0:T(8,128)(2,1)}, u32[]{:S(2)}) copy-start(bf16[640,128]{1,0:T(8,128)(2,1)} %param.8) | copy-start | bytes 491524
  7.2 46.7 %reduce-scatter.2.cloned.1.call-start = ((), (), s32[]{:S(2)}) async-start(), calls=%async_computation.1 | async-start | bytes 1474560 | tf_op jit(solution)/shard_map/reduce_scatter | solution.py:54
  15.4 72.1 %copy-start.1 = (f32[1024,128]{1,0:T(8,128)S(1)}, f32[1024,128]{1,0:T(8,128)}, u32[]{:S(2)}) copy-start(f32[1024,128]{1,0:T(8,128)} %param.9) | copy-start | bytes 1572868
  15.4 65.4 %all-gather.2.cloned.1.call-start = ((), (), s32[]{:S(2)}) async-start(), calls=%async_computation.2 | async-start | bytes 1474560 | tf_op jit(solution)/shard_map/all_gather | solution.py:64
  55.6 32.1 %copy-start.5 = (f32[128]{0:T(128)S(1)}, f32[128]{0:T(128)}, u32[]{:S(2)}) copy-start(f32[128]{0:T(128)} %param.10) | copy-start | bytes 1540
  55.6 68.7 %copy-start.2 = (bf16[1024,512]{1,0:T(8,128)(2,1)S(1)}, bf16[1024,512]{1,0:T(8,128)(2,1)}, u32[]{:S(2)}) copy-start(bf16[1024,512]{1,0:T(8,128)(2,1)} %param.13) | copy-start | bytes 3145732
  55.7 67.6 %all-reduce.2.cloned.1.call-start = ((), (), s32[]{:S(2)}) async-start(), calls=%async_computation.3 | async-start | bytes 524288 | tf_op jit(solution)/shard_map/psum | solution.py:68
  124.7 4.4 %copy-start.3 = (f32[2,512,128]{1,2,0:T(8,128)}, f32[2,512,128]{1,2,0:T(8,128)S(1)}, u32[]{:S(2)}) copy-start(f32[2,512,128]{1,2,0:T(8,128)S(1)} %convolution_bitcast_fusion.2) | copy-start | bytes 1572868
  125.4 6.9 %collective-permute-start = (bf16[512,128]{0,1:T(8,128)(2,1)}, bf16[512,128]{0,1:T(8,128)(2,1)S(1)}, u32[]{:S(2)}, u32[]{:S(2)}) collective-permute-start(bf16[512,128]{0,1:T(8,128)(2,1)} %fusion.16), channel_id=1, source_target_pairs={{1,0},{2,1},{3,2},{4,3},{5,4},{6,5},{7,6},{9,8},{10,9},{11,10},{12... | collective-permute-start | bytes 393224 | tf_op jit(solution)/shard_map/ppermute | solution.py:14
  132.7 7.2 %collective-permute-start.1 = (bf16[512,128]{0,1:T(8,128)(2,1)S(1)}, bf16[512,128]{0,1:T(8,128)(2,1)S(1)}, u32[]{:S(2)}, u32[]{:S(2)}) collective-permute-start(bf16[512,128]{0,1:T(8,128)(2,1)S(1)} %get-tuple-element.4), channel_id=1, source_target_pairs={{0,1},{1,2},{2,3},{3,4},{4,5},{5,6},{6,7},{8,9},{9,10},{10,11},{11... | collective-permute-start | bytes 393224 | tf_op jit(solution)/shard_map/ppermute | solution.py:14
Sparse Core Ops, SparseCore 0:
  15.5 38.3 reduce-scatter.1
  56.3 24.4 all-gather.1
  87.6 35.6 all-reduce.1
where the time goes:
time: 148 us
  waiting for transfers between devices  102 us (69%)
  matrix products  17.4 us (12%)
  between operations  13.9 us (9%)
  local copies, waits for them, and re-layouts  5.14 us (3%)
  other arithmetic  4.63 us (3%)
  starting transfers between devices  4.44 us (3%)
    reduce_scatter x1, waiting for transfers between devices, local(): lax.psum_scatter(jnp.dot(row_block, coef_half, preferred_element_type=jnp...  38.4 us
    psum x1, waiting for transfers between devices, local(): lax.psum(grad_part.astype(jnp.bfloat16), 'person').astype(jnp.float32)  35.5 us
    all_gather x1, waiting for transfers between devices, local(): lax.all_gather(residual.astype(jnp.bfloat16), 'variant', axis=0, tiled=True)  25.1 us
    dot_general x1, matrix products, local(): jnp.dot(row_block, coef_half, preferred_element_type=jnp.float32)  8.11 us
    dot_general x1, matrix products, local(): lax.dot_general(row_block, lax.all_gather(residual.astype(jnp.bfloat16),...  6.65 us
    ppermute x2, starting transfers between devices, shifted(): return lax.ppermute(block, axis, route)  4.32 us
    ppermute x2, waiting for transfers between devices, shifted(): return lax.ppermute(block, axis, route)  3.24 us
  transfers between devices with their start and end apart: 5, of which 4 were waited for; matrix products, arithmetic and copies ran while one was open for 5% of the time, Pallas kernels for 0%

commit v1 on v0

v1 whole, which is shorter than its diff:
```python
import functools
import math
import types

import jax
import jax.numpy as jnp
from jax import lax
from jax.experimental import pallas as pl
from jax.experimental.pallas import tpu as pltpu
from jax.sharding import PartitionSpec as P

step_size = 0.25
MESH = pl.DeviceIdType.MESH
CHUNKS = 4
F32 = jnp.float32
BF16 = jnp.bfloat16


def log2(n):
    return n.bit_length() - 1


def kernel(n, persons, names, x_hbm, y_hbm, coef_hbm, prec_hbm, noise_hbm, d_hbm, e_hbm, prop_hbm, res_hbm, *scratch):
    s = types.SimpleNamespace(**dict(zip(names, scratch)))
    xv, y, coef, coef_h, prec = s.x, s.y, s.coef, s.coef_h, s.prec
    d, e, noise = s.d, s.e, s.noise
    chunks, _, m, rc, variants = xv.shape
    traits = coef.shape[1]
    groups, _, cw = s.acc.shape
    blocks, _, band = s.pulled.shape
    chip_bits = log2(m)
    inverse_root = 1.0 / math.sqrt(variants * n)
    half = persons // 2

    v = lax.axis_index("variant")
    p = lax.axis_index("person")
    chip = lax.div(v, 2)
    core = v - 2 * chip
    other = 1 - core
    mate = v + 1 - 2 * core
    bit = [lax.rem(lax.div(chip, 1 << k), 2) for k in range(chip_bits)]
    weight = [other * (1 << k) + core * (1 << (chip_bits - 1 - k)) for k in range(chip_bits)]
    mine = [other * bit[k] + core * bit[chip_bits - 1 - k] for k in range(chip_bits)]
    partner = [(chip + weight[k] * (1 - 2 * mine[k])) * 2 + core for k in range(chip_bits)]

    def place(rel):
        total = 0 * chip
        for k in range(chip_bits):
            total = total + (1 - mine[k] if (rel >> k) & 1 else mine[k]) * weight[k]
        return total

    where = [place(rel) for rel in range(m)]

    def remote(src, dst, send, recv, variant=None, person=None):
        target = {"variant": variant} if person is None else {"person": person}
        return pltpu.make_async_remote_copy(
            src_ref=src, dst_ref=dst, send_sem=send, recv_sem=recv, device_id=target, device_id_type=MESH
        )

    sent = []

    def send(*args, **kw):
        copy = remote(*args, **kw)
        copy.start()
        sent.append(copy)

    loads = {}

    def load(key, src, dst):
        copy = pltpu.make_async_copy(src, dst, s.load_sem.at[len(loads)])
        copy.start()
        loads[key] = copy

    load("coef", coef_hbm, coef)
    for c in range(chunks):
        load(("x", c, 0), x_hbm.at[:, other, pl.ds(c * rc, rc), :], xv.at[c, 0])
        load(("x", c, 1), x_hbm.at[:, core, pl.ds(c * rc, rc), :], xv.at[c, 1])
    load("y", y_hbm, y)
    load("prec", prec_hbm, prec)
    load("noise", noise_hbm, noise)
    load("d", d_hbm, d)
    load("e", e_hbm, e)

    barrier = pltpu.get_barrier_semaphore()
    greeted = 1 + chip_bits
    for who in [mate] + partner:
        pl.semaphore_signal(barrier, inc=1, device_id={"variant": who}, device_id_type=MESH)

    def greet(ok, target):
        @pl.when(ok)
        def _():
            pl.semaphore_signal(barrier, inc=1, device_id=target, device_id_type=MESH)

    across = v - 1 + 2 * core
    checks = [
        (jnp.logical_and(across >= 0, across < n), {"variant": across}),
        (p > 0, {"person": p - 1}),
        (p < persons - 1, {"person": p + 1}),
    ]
    peers = greeted
    for ok, target in checks:
        greet(ok, target)
        peers = peers + ok.astype(jnp.int32)

    def barrier_wait():
        pl.semaphore_wait(barrier, peers)

    offset = [m - (m >> k) for k in range(chip_bits + 1)]

    def predict(c, t):
        loads["x", c, t].wait()
        rows = xv[c, t].reshape(m * rc, variants)
        return jnp.dot(rows, coef_h[...], preferred_element_type=F32).reshape(m, rc, traits)

    def swap(c):
        return remote(s.swap_out.at[c], s.swap_in.at[c], s.swap_send.at[c], s.swap_recv.at[c], variant=mate)

    def stage_predict(c):
        if c == 0:
            loads["coef"].wait()
            coef_h[...] = coef[...].astype(BF16)
        s.swap_out[c] = predict(c, 0).astype(BF16)
        if c == 0:
            barrier_wait()
        copy = swap(c)
        copy.start()
        sent.append(copy)
        s.sum[c] = predict(c, 1)

    def give(c, k, j, value):
        slot = offset[k] + j
        s.part_out[c, slot] = value.astype(BF16)
        send(s.part_out.at[c, slot], s.part_in.at[c, slot], s.part_send.at[c, slot],
             s.part_recv.at[c, slot], variant=partner[k])

    def finish(c, value):
        if c == 0:
            loads["y"].wait()
        rows = pl.ds(c * rc, rc)
        residual = y[rows, :].astype(F32) - value * inverse_root
        s.res[rows, :] = residual
        copy = pltpu.make_async_copy(s.res.at[rows, :], res_hbm.at[rows, :], s.out_sem.at[c])
        copy.start()
        outs.append(copy)
        s.half[c, 1, chip] = residual.astype(BF16)
        forward(c, 0)

    outs = []

    def stage_reduce(c, k):
        if k == 0:
            swap(c).wait_recv()
        count = m >> k
        order = [j for j in reversed(range(count)) if j % 2] + [j for j in reversed(range(count)) if j % 2 == 0]
        for j in order:
            spot = where[j << k]
            if k == 0:
                got = s.swap_in[c, spot]
            else:
                slot = offset[k - 1] + j
                remote(s.part_out.at[c, slot], s.part_in.at[c, slot], s.part_send.at[c, slot],
                       s.part_recv.at[c, slot], variant=partner[k - 1]).wait_recv()
                got = s.part_in[c, slot]
            value = s.sum[c, spot] + got.astype(F32)
            if k == chip_bits:
                finish(c, value)
            elif j % 2:
                give(c, k, j >> 1, value)
            else:
                s.sum[c, spot] = value

    def low(rel):
        return chip_bits if rel == 0 else (rel & -rel).bit_length() - 1

    gather_slot = {}

    def forward(c, rel):
        spot = where[rel]
        piece = s.half.at[c, 1, spot]
        for k in reversed(range(low(rel))):
            slot = gather_slot.setdefault((rel, k), len(gather_slot))
            send(piece, piece, s.half_send.at[c, slot], s.half_recv.at[c, 1, spot], variant=partner[k])
        slot = gather_slot.setdefault((rel, -1), len(gather_slot))
        send(piece, s.half.at[c, 0, spot], s.half_send.at[c, slot], s.half_recv.at[c, 0, spot], variant=mate)

    def arrived(c, t, spot, who):
        piece = s.half.at[c, t, spot]
        remote(piece, piece, s.half_send.at[c, 0], s.half_recv.at[c, t, spot], variant=who).wait_recv()

    def stage_gather(c, k):
        for rel in range(1, m):
            if low(rel) == k:
                arrived(c, 1, where[rel], partner[k])
                forward(c, rel)

    def stage_gradient(c):
        for w in range(m):
            arrived(c, 0, w, mate)
        turned = s.half[c].reshape(n * rc, traits).T
        for z in range(groups):
            cols = pl.ds(z * cw, cw)
            part = jnp.dot(turned, xv[c, :, :, :, cols].reshape(n * rc, cw), preferred_element_type=F32)
            if c:
                part = part + s.acc[z]
            s.acc[z] = part
            if c == chunks - 1:
                start_sum(z)

    side = lax.div(p, max(half, 1))
    dist = (1 - side) * (half - 1 - p) + side * (p - half)
    inward = p + 1 - 2 * side
    outward = p - 1 + 2 * side
    outer = dist < half - 1
    centre = dist == 0
    edge = dist > 0

    def to_inner(z):
        return remote(s.own.at[z], s.inner.at[z], s.inner_send.at[z], s.inner_recv.at[z], person=inward)

    def to_cross(z):
        return remote(s.own.at[z], s.cross.at[z], s.cross_send.at[z], s.cross_recv.at[z], person=inward)

    def to_outer(z):
        return remote(s.tot.at[z], s.tot.at[z], s.tot_send.at[z], s.tot_recv.at[z], person=outward)

    def send_inward(z):
        s.own[z] = s.acc[z].astype(BF16)
        @pl.when(edge)
        def _():
            to_inner(z).start()
        @pl.when(centre)
        def _():
            to_cross(z).start()

    def start_sum(z):
        if persons == 1:
            s.tot[z] = s.acc[z].astype(BF16)
            return
        @pl.when(jnp.logical_not(outer))
        def _():
            send_inward(z)

    def join_sum(z):
        @pl.when(outer)
        def _():
            to_inner(z).wait_recv()
            s.acc[z] = s.acc[z] + s.inner[z].astype(F32)
            send_inward(z)

    def cross_sum(z):
        @pl.when(centre)
        def _():
            to_cross(z).wait_recv()
            s.tot[z] = (s.own[z].astype(F32) + s.cross[z].astype(F32)).astype(BF16)
            @pl.when(outer)
            def _():
                to_outer(z).start()

    def take_sum(z):
        @pl.when(edge)
        def _():
            to_outer(z).wait_recv()
            @pl.when(outer)
            def _():
                to_outer(z).start()

    def up_copy():
        return remote(s.up_out, s.up_in, s.edge_send.at[0], s.edge_recv.at[0], variant=v - 1)

    def carry_copy():
        return remote(s.carry_out, s.carry_in, s.edge_send.at[1], s.edge_recv.at[1], variant=v + 1)

    def rows_of(j):
        return pl.ds(j * band, band)

    def block_gradient(j):
        grad = jnp.concatenate([s.grad[z] for z in range(j * band // cw, (j + 1) * band // cw)], 1)
        upward = jnp.dot(grad, e[rows_of(j), :], preferred_element_type=F32)
        if j == 0:
            @pl.when(v > 0)
            def _():
                s.up_out[...] = upward.astype(BF16)
                up_copy().start()
        else:
            s.pulled[j - 1] = s.pulled[j - 1] + upward
        s.pulled[j] = jnp.dot(grad, d[rows_of(j), :], preferred_element_type=F32)

    def block_update(j):
        value = step_size / 2.0 * s.pulled[j].T + math.sqrt(step_size) * noise[rows_of(j), :].astype(F32)
        return value.astype(BF16)

    def store_out(j):
        copy = pltpu.make_async_copy(s.prop.at[rows_of(j), :], prop_hbm.at[rows_of(j), :], s.out_sem.at[chunks + j])
        copy.start()
        outs.append(copy)

    stages = [stage_predict]
    stages += [functools.partial(stage_reduce, k=k) for k in range(chip_bits + 1)]
    stages += [functools.partial(stage_gather, k=k) for k in reversed(range(chip_bits))]
    stages += [stage_gradient]
    for slot in range(chunks + len(stages) - 1):
        for position, stage in enumerate(stages):
            if 0 <= slot - position < chunks:
                stage(slot - position)
        if slot == chunks - 1:
            loads["prec"].wait()
            spread = jnp.broadcast_to(prec[...], (traits, traits)).T
            s.prec_t[...] = spread * inverse_root
            for z in range(groups):
                s.coef_t[z] = coef[pl.ds(z * cw, cw), :].T
    for key in ("noise", "d", "e"):
        loads[key].wait()

    if persons > 1:
        for z in range(groups):
            join_sum(z)
            if z:
                cross_sum(z - 1)
        cross_sum(groups - 1)
    scale = jnp.concatenate([s.prec_t[...]] * (cw // traits), 1)
    for z in range(groups):
        if persons > 1:
            take_sum(z)
        s.grad[z] = (s.tot[z].astype(F32) * scale - s.coef_t[z]).astype(BF16)
        if (z + 1) * cw % band == 0:
            block_gradient((z + 1) * cw // band - 1)

    @pl.when(v < n - 1)
    def _():
        up_copy().wait_recv()
        s.pulled[blocks - 1] = s.pulled[blocks - 1] + s.up_in[...].astype(F32)

    s.carry_out[...] = block_update(blocks - 1)

    @pl.when(v < n - 1)
    def _():
        carry_copy().start()

    before = None
    for j in range(blocks):
        now = s.carry_out[...] if j == blocks - 1 else block_update(j)
        value = coef[rows_of(j), :] + jnp.dot(d[rows_of(j), :], now, preferred_element_type=F32)
        if j:
            value = value + jnp.dot(e[rows_of(j), :], before, preferred_element_type=F32)
        s.prop[rows_of(j), :] = value
        if j:
            store_out(j)
        before = now

    @pl.when(v > 0)
    def _():
        carry_copy().wait_recv()
        s.prop[rows_of(0), :] = s.prop[rows_of(0), :] + jnp.dot(
            e[rows_of(0), :], s.carry_in[...], preferred_element_type=F32
        )

    store_out(0)

    for copy in sent:
        copy.wait_send()
    if persons > 1:
        for z in range(groups):
            @pl.when(edge)
            def _():
                to_inner(z).wait_send()
            @pl.when(centre)
            def _():
                to_cross(z).wait_send()
            @pl.when(outer)
            def _():
                to_outer(z).wait_send()

    @pl.when(v > 0)
    def _():
        up_copy().wait_send()

    @pl.when(v < n - 1)
    def _():
        carry_copy().wait_send()

    for copy in outs:
        copy.wait()


def local(n, persons, dosages, phenotypes, coefficients, trait_precision, noise, band_diag, band_lower):
    people, variants = dosages.shape
    rows, traits = phenotypes.shape
    band = band_diag.shape[1]
    blocks = variants // band
    m = n // 2
    chunks = CHUNKS
    rc = rows // chunks
    cw = 256
    groups = variants // cw
    dma = pltpu.SemaphoreType.DMA
    scratch = dict(
        x=pltpu.VMEM((chunks, 2, m, rc, variants), BF16),
        y=pltpu.VMEM((rows, traits), BF16),
        coef=pltpu.VMEM((variants, traits), F32),
        coef_h=pltpu.VMEM((variants, traits), BF16),
        prec=pltpu.VMEM((1, traits), F32),
        noise=pltpu.VMEM((variants, traits), BF16),
        d=pltpu.VMEM((variants, band), BF16),
        e=pltpu.VMEM((variants, band), BF16),
        swap_out=pltpu.VMEM((chunks, m, rc, traits), BF16),
        swap_in=pltpu.VMEM((chunks, m, rc, traits), BF16),
        sum=pltpu.VMEM((chunks, m, rc, traits), F32),
        part_out=pltpu.VMEM((chunks, m, rc, traits), BF16),
        part_in=pltpu.VMEM((chunks, m, rc, traits), BF16),
        res=pltpu.VMEM((rows, traits), F32),
        half=pltpu.VMEM((chunks, 2, m, rc, traits), BF16),
        acc=pltpu.VMEM((groups, traits, cw), F32),
        own=pltpu.VMEM((groups, traits, cw), BF16),
        inner=pltpu.VMEM((groups, traits, cw), BF16),
        cross=pltpu.VMEM((groups, traits, cw), BF16),
        tot=pltpu.VMEM((groups, traits, cw), BF16),
        grad=pltpu.VMEM((groups, traits, cw), BF16),
        coef_t=pltpu.VMEM((groups, traits, cw), F32),
        prec_t=pltpu.VMEM((traits, traits), F32),
        pulled=pltpu.VMEM((blocks, traits, band), F32),
        up_out=pltpu.VMEM((traits, band), BF16),
        up_in=pltpu.VMEM((traits, band), BF16),
        carry_out=pltpu.VMEM((band, traits), BF16),
        carry_in=pltpu.VMEM((band, traits), BF16),
        prop=pltpu.VMEM((variants, traits), F32),
        load_sem=dma((2 * chunks + 6,)),
        swap_send=dma((chunks,)),
        swap_recv=dma((chunks,)),
        part_send=dma((chunks, m)),
        part_recv=dma((chunks, m)),
        half_send=dma((chunks, 2 * m)),
        half_recv=dma((chunks, 2, m)),
        inner_send=dma((groups,)),
        inner_recv=dma((groups,)),
        cross_send=dma((groups,)),
        cross_recv=dma((groups,)),
        tot_send=dma((groups,)),
        tot_recv=dma((groups,)),
        edge_send=dma((2,)),
        edge_recv=dma((2,)),
        out_sem=dma((chunks + blocks,)),
    )
    anywhere = pl.BlockSpec(memory_space=pl.ANY)
    return pl.pallas_call(
        functools.partial(kernel, n, persons, tuple(scratch)),
        out_shape=(
            jax.ShapeDtypeStruct((variants, traits), F32),
            jax.ShapeDtypeStruct((rows, traits), F32),
        ),
        in_specs=[anywhere] * 7,
        out_specs=(anywhere, anywhere),
        scratch_shapes=list(scratch.values()),
        compiler_params=pltpu.CompilerParams(
            collective_id=0, has_side_effects=True, vmem_limit_bytes=60 * 1024 * 1024
        ),
    )(
        dosages.reshape(m, 2, rows, variants),
        phenotypes,
        coefficients,
        trait_precision.reshape(1, traits),
        noise,
        band_diag,
        band_lower,
    )


def solution(mesh):
    n, persons = mesh.shape["variant"], mesh.shape["person"]
    placed = (
        P("person", "variant"),
        P(("person", "variant"), None),
        P("variant", None),
        P(),
        P("variant", None),
        P("variant", None),
        P("variant", None),
    )
    return jax.shard_map(
        functools.partial(local, n, persons),
        mesh=mesh,
        in_specs=placed,
        out_specs=(P("variant", None), P(("person", "variant"), None)),
        check_vma=False,
    )
```

time: 148 us -> 54.5 us (0.37)
  waiting for transfers between devices: 102 us -> 0 us
  Pallas kernels: 0 us -> 50.1 us
  matrix products: 17.4 us -> 0 us
  between operations: 13.9 us -> 0.64 us
  other arithmetic: 4.63 us -> 0 us
  starting transfers between devices: 4.44 us -> 0 us
  local copies, waits for them, and re-layouts: 5.14 us -> 3.59 us
    pallas_call x0 -> x1, Pallas kernels: none -> 50.1 us  [local(): pl.pallas_call(functools.partial(kernel, n, persons, tuple(scratch)), out...]
    reduce_scatter x1 -> x0, waiting for transfers between devices: 38.4 us -> none  [local(): lax.psum_scatter(jnp.dot(row_block, coef_half, preferred_element_type=jnp...]
    psum x1 -> x0, waiting for transfers between devices: 35.5 us -> none  [local(): lax.psum(grad_part.astype(jnp.bfloat16), 'person').astype(jnp.float32)]
    all_gather x1 -> x0, waiting for transfers between devices: 25.1 us -> none  [local(): lax.all_gather(residual.astype(jnp.bfloat16), 'variant', axis=0, tiled=True)]
    dot_general x6 -> x0, matrix products: 17.4 us -> none  [the longest x1 8.11 us: local(): jnp.dot(row_block, coef_half, preferred_element_type=jnp.float32)]
    ppermute x2 -> x0, starting transfers between devices: 4.32 us -> none  [shifted(): return lax.ppermute(block, axis, route)]
    unnamed x13 -> x2, local copies, waits for them, and re-layouts: 0.23 us -> 3.59 us
    ppermute x2 -> x0, waiting for transfers between devices: 3.24 us -> none  [shifted(): return lax.ppermute(block, axis, route)]
  transfers between devices with their start and end apart: 5 -> 0, of which waited for: 4 -> 0; matrix products, arithmetic and copies ran while one was open for 5% -> 0% of each run, Pallas kernels for 0% -> 0%
where the time goes in v1:
time: 54.5 us; the launch traced here: 54.3 us
  Pallas kernels  50.1 us (92%)
  local copies, waits for them, and re-layouts  3.59 us (7%)
  between operations  0.64 us (1%)
    pallas_call x1, Pallas kernels, local(): pl.pallas_call(functools.partial(kernel, n, persons, tuple(scratch)), out...  50.1 us
    unnamed x2, local copies, waits for them, and re-layouts  3.59 us

profile of v1, /device:TPU:4, one launch (start us, length us, event | category | flops | bytes accessed | tf_op | source)
XLA Modules:
  0.0 54.3 jit_solution(789825484636228522)
XLA Ops:
  0.6 50.1 %shard_map.86 = (f32[1024,128]{1,0:T(8,128)}, f32[640,128]{1,0:T(8,128)}) custom-call(bf16[4,2,640,1024]{3,2,1,0:T(8,128)(2,1)} %bitcast.2, bf16[640,128]{1,0:T(8,128)(2,1)} %y_hbm.1, f32[1024,128]{1,0:T(8,128)} %coef_hbm.1, f32[1,128]{1,0:T(1,128)} %bitcast.3, bf16[1024,128]{1,0:T(8,128)(2,1)} %noise_hbm.1, bf16[1024,512]{1,0:T(8,128)(2,1)} %d_hbm.1, ...), custom_call_target="tpu_custom_call" | custom-call | tf_op jit(solution)/shard_map/pallas_call | solution.py:444
  50.7 1.9 %copy.11 = f32[1024,128]{1,0:T(8,128)} copy(f32[1024,128]{1,0:T(8,128)} %get-tuple-element.4) | data formatting | bytes 1048576
  52.6 1.7 %copy.12 = f32[640,128]{1,0:T(8,128)} copy(f32[640,128]{1,0:T(8,128)} %get-tuple-element.5) | data formatting | bytes 655360

commit v2 on v1

--- a/solution.py
+++ b/solution.py
@@ -12,6 +12,11 @@
 step_size = 0.25
 MESH = pl.DeviceIdType.MESH
 CHUNKS = 4
+NEAR = 1
+FAR = 2
+TAIL = True
+GRANT = 60
+GROUP = 256
 F32 = jnp.float32
 BF16 = jnp.bfloat16
 
@@ -298,10 +303,12 @@
     stages += [functools.partial(stage_reduce, k=k) for k in range(chip_bits + 1)]
     stages += [functools.partial(stage_gather, k=k) for k in reversed(range(chip_bits))]
     stages += [stage_gradient]
-    for slot in range(chunks + len(stages) - 1):
-        for position, stage in enumerate(stages):
-            if 0 <= slot - position < chunks:
-                stage(slot - position)
+    starts = [0, NEAR] + [NEAR + FAR * (k + 1) for k in range(2 * chip_bits)]
+    starts.append(starts[-1] + NEAR)
+    for slot in range(chunks + starts[-1]):
+        for start, stage in zip(starts, stages):
+            if 0 <= slot - start < chunks:
+                stage(slot - start)
         if slot == chunks - 1:
             loads["prec"].wait()
             spread = jnp.broadcast_to(prec[...], (traits, traits)).T
@@ -382,6 +389,18 @@
         copy.wait()
 
 
+def hand_over(a_in, b_in, a_out, b_out, a, b, sem):
+    loads = [pltpu.make_async_copy(a_in, a, sem.at[0]), pltpu.make_async_copy(b_in, b, sem.at[1])]
+    stores = [pltpu.make_async_copy(a, a_out, sem.at[2]), pltpu.make_async_copy(b, b_out, sem.at[3])]
+    for copy in loads:
+        copy.start()
+    for load, store in zip(loads, stores):
+        load.wait()
+        store.start()
+    for copy in stores:
+        copy.wait()
+
+
 def local(n, persons, dosages, phenotypes, coefficients, trait_precision, noise, band_diag, band_lower):
     people, variants = dosages.shape
     rows, traits = phenotypes.shape
@@ -390,7 +409,7 @@
     m = n // 2
     chunks = CHUNKS
     rc = rows // chunks
-    cw = 256
+    cw = GROUP
     groups = variants // cw
     dma = pltpu.SemaphoreType.DMA
     scratch = dict(
@@ -440,18 +459,19 @@
         edge_recv=dma((2,)),
         out_sem=dma((chunks + blocks,)),
     )
+    made_shape = (
+        jax.ShapeDtypeStruct((variants, traits), F32),
+        jax.ShapeDtypeStruct((rows, traits), F32),
+    )
     anywhere = pl.BlockSpec(memory_space=pl.ANY)
-    return pl.pallas_call(
+    made = pl.pallas_call(
         functools.partial(kernel, n, persons, tuple(scratch)),
-        out_shape=(
-            jax.ShapeDtypeStruct((variants, traits), F32),
-            jax.ShapeDtypeStruct((rows, traits), F32),
-        ),
+        out_shape=made_shape,
         in_specs=[anywhere] * 7,
         out_specs=(anywhere, anywhere),
         scratch_shapes=list(scratch.values()),
         compiler_params=pltpu.CompilerParams(
-            collective_id=0, has_side_effects=True, vmem_limit_bytes=60 * 1024 * 1024
+            collective_id=0, has_side_effects=True, vmem_limit_bytes=GRANT * 1024 * 1024
         ),
     )(
         dosages.reshape(m, 2, rows, variants),
@@ -462,6 +482,20 @@
         band_diag,
         band_lower,
     )
+    if not TAIL:
+        return made
+    return pl.pallas_call(
+        hand_over,
+        out_shape=made_shape,
+        in_specs=[anywhere] * 2,
+        out_specs=(anywhere, anywhere),
+        scratch_shapes=[
+            pltpu.VMEM((variants, traits), F32),
+            pltpu.VMEM((rows, traits), F32),
+            dma((4,)),
+        ],
+        compiler_params=pltpu.CompilerParams(vmem_limit_bytes=4 * 1024 * 1024),
+    )(*made)
 
 
 def solution(mesh):

time: 54.5 us -> 52.1 us (0.956)
  local copies, waits for them, and re-layouts: 3.59 us -> 2.01 us
  Pallas kernels: 50.1 us -> 49.2 us
    pallas_call x1, Pallas kernels: 50.1 us -> 48.2 us  [local(): pl.pallas_call(functools.partial(kernel, n, persons, tuple(scratch)), out...]
    unnamed x2 -> x4, local copies, waits for them, and re-layouts: 3.59 us -> 2.01 us
    pallas_call x0 -> x1, Pallas kernels: none -> 1.06 us  [local(): pl.pallas_call(hand_over, out_shape=made_shape, in_specs=[anywhere] * 2,...]
where the time goes in v2:
time: 52.1 us; the launch traced here: 51.9 us
  Pallas kernels  49.2 us (94%)
  local copies, waits for them, and re-layouts  2.01 us (4%)
  between operations  0.65 us (1%)
    pallas_call x1, Pallas kernels, local(): pl.pallas_call(functools.partial(kernel, n, persons, tuple(scratch)), out...  48.2 us
    unnamed x4, local copies, waits for them, and re-layouts  2.01 us
    pallas_call x1, Pallas kernels, local(): pl.pallas_call(hand_over, out_shape=made_shape, in_specs=[anywhere] * 2,...  1.06 us

profile of v2, /device:TPU:4, one launch (start us, length us, event | category | flops | bytes accessed | tf_op | source)
XLA Modules:
  0.0 51.9 jit_solution(16299463832930688211)
XLA Ops:
  0.6 48.2 %shard_map.86 = (f32[1024,128]{1,0:T(8,128)}, f32[640,128]{1,0:T(8,128)}) custom-call(bf16[4,2,640,1024]{3,2,1,0:T(8,128)(2,1)} %bitcast.2, bf16[640,128]{1,0:T(8,128)(2,1)} %y_hbm.1, f32[1024,128]{1,0:T(8,128)} %coef_hbm.1, f32[1,128]{1,0:T(1,128)} %bitcast.3, bf16[1024,128]{1,0:T(8,128)(2,1)} %noise_hbm.1, bf16[1024,512]{1,0:T(8,128)(2,1)} %d_hbm.1, ...), custom_call_target="tpu_custom_call" | custom-call | tf_op jit(solution)/shard_map/pallas_call | solution.py:467
  48.8 0.0 copy-start
  48.8 1.0 %copy-done = f32[1024,128]{1,0:T(8,128)S(1)} copy-done((f32[1024,128]{1,0:T(8,128)S(1)}, f32[1024,128]{1,0:T(8,128)}, u32[]{:S(2)}) %copy-start) | copy-done | bytes 524312
  49.9 0.0 copy-start.1
  49.9 1.0 %copy-done.1 = f32[640,128]{1,0:T(8,128)S(1)} copy-done((f32[640,128]{1,0:T(8,128)S(1)}, f32[640,128]{1,0:T(8,128)}, u32[]{:S(2)}) %copy-start.1) | copy-done | bytes 327704
  50.8 1.1 %shard_map.87 = (f32[1024,128]{1,0:T(8,128)}, f32[640,128]{1,0:T(8,128)}) custom-call(f32[1024,128]{1,0:T(8,128)S(1)} %copy-done, f32[640,128]{1,0:T(8,128)S(1)} %copy-done.1), custom_call_target="tpu_custom_call" | custom-call | tf_op jit(solution)/shard_map/pallas_call | solution.py:487
Async XLA Ops:
  48.8 1.0 %copy-start = (f32[1024,128]{1,0:T(8,128)S(1)}, f32[1024,128]{1,0:T(8,128)}, u32[]{:S(2)}) copy-start(f32[1024,128]{1,0:T(8,128)} %get-tuple-element.4.a_in) | copy-start | bytes 1572868
  49.9 1.0 %copy-start.1 = (f32[640,128]{1,0:T(8,128)S(1)}, f32[640,128]{1,0:T(8,128)}, u32[]{:S(2)}) copy-start(f32[640,128]{1,0:T(8,128)} %get-tuple-element.5.b_in) | copy-start | bytes 983044

commit v3 on v2

--- a/solution.py
+++ b/solution.py
@@ -219,17 +219,22 @@
     centre = dist == 0
     edge = dist > 0
 
+    pieces = 2 * groups
+
+    def spot(q):
+        return q // 2, pl.ds((q % 2) * (traits // 2), traits // 2), slice(None)
+
     def to_inner(z):
-        return remote(s.own.at[z], s.inner.at[z], s.inner_send.at[z], s.inner_recv.at[z], person=inward)
+        return remote(s.own.at[spot(z)], s.inner.at[spot(z)], s.inner_send.at[z], s.inner_recv.at[z], person=inward)
 
     def to_cross(z):
-        return remote(s.own.at[z], s.cross.at[z], s.cross_send.at[z], s.cross_recv.at[z], person=inward)
+        return remote(s.own.at[spot(z)], s.cross.at[spot(z)], s.cross_send.at[z], s.cross_recv.at[z], person=inward)
 
     def to_outer(z):
-        return remote(s.tot.at[z], s.tot.at[z], s.tot_send.at[z], s.tot_recv.at[z], person=outward)
+        return remote(s.tot.at[spot(z)], s.tot.at[spot(z)], s.tot_send.at[z], s.tot_recv.at[z], person=outward)
 
     def send_inward(z):
-        s.own[z] = s.acc[z].astype(BF16)
+        s.own[spot(z)] = s.acc[spot(z)].astype(BF16)
         @pl.when(edge)
         def _():
             to_inner(z).start()
@@ -243,20 +248,21 @@
             return
         @pl.when(jnp.logical_not(outer))
         def _():
-            send_inward(z)
+            send_inward(2 * z)
+            send_inward(2 * z + 1)
 
     def join_sum(z):
         @pl.when(outer)
         def _():
             to_inner(z).wait_recv()
-            s.acc[z] = s.acc[z] + s.inner[z].astype(F32)
+            s.acc[spot(z)] = s.acc[spot(z)] + s.inner[spot(z)].astype(F32)
             send_inward(z)
 
     def cross_sum(z):
         @pl.when(centre)
         def _():
             to_cross(z).wait_recv()
-            s.tot[z] = (s.own[z].astype(F32) + s.cross[z].astype(F32)).astype(BF16)
+            s.tot[spot(z)] = (s.own[spot(z)].astype(F32) + s.cross[spot(z)].astype(F32)).astype(BF16)
             @pl.when(outer)
             def _():
                 to_outer(z).start()
@@ -319,15 +325,17 @@
         loads[key].wait()
 
     if persons > 1:
-        for z in range(groups):
+        for z in range(pieces):
             join_sum(z)
-            if z:
-                cross_sum(z - 1)
-        cross_sum(groups - 1)
+            if z > 1:
+                cross_sum(z - 2)
+        cross_sum(pieces - 2)
+        cross_sum(pieces - 1)
     scale = jnp.concatenate([s.prec_t[...]] * (cw // traits), 1)
     for z in range(groups):
         if persons > 1:
-            take_sum(z)
+            take_sum(2 * z)
+            take_sum(2 * z + 1)
         s.grad[z] = (s.tot[z].astype(F32) * scale - s.coef_t[z]).astype(BF16)
         if (z + 1) * cw % band == 0:
             block_gradient((z + 1) * cw // band - 1)
@@ -366,7 +374,7 @@
     for copy in sent:
         copy.wait_send()
     if persons > 1:
-        for z in range(groups):
+        for z in range(pieces):
             @pl.when(edge)
             def _():
                 to_inner(z).wait_send()
@@ -449,12 +457,12 @@
         part_recv=dma((chunks, m)),
         half_send=dma((chunks, 2 * m)),
         half_recv=dma((chunks, 2, m)),
-        inner_send=dma((groups,)),
-        inner_recv=dma((groups,)),
-        cross_send=dma((groups,)),
-        cross_recv=dma((groups,)),
-        tot_send=dma((groups,)),
-        tot_recv=dma((groups,)),
+        inner_send=dma((2 * groups,)),
+        inner_recv=dma((2 * groups,)),
+        cross_send=dma((2 * groups,)),
+        cross_recv=dma((2 * groups,)),
+        tot_send=dma((2 * groups,)),
+        tot_recv=dma((2 * groups,)),
         edge_send=dma((2,)),
         edge_recv=dma((2,)),
         out_sem=dma((chunks + blocks,)),

time: 52.1 us -> 52.4 us (level)
  the two profiles are of different devices: /device:TPU:4 before, /device:TPU:12 now
where the time goes in v3:
time: 52.4 us; the launch traced here: 52.2 us
  Pallas kernels  49.5 us (94%)
  local copies, waits for them, and re-layouts  2.01 us (4%)
  between operations  0.65 us (1%)
    pallas_call x1, Pallas kernels, local(): pl.pallas_call(functools.partial(kernel, n, persons, tuple(scratch)), out...  48.5 us
    unnamed x4, local copies, waits for them, and re-layouts  2.01 us
    pallas_call x1, Pallas kernels, local(): pl.pallas_call(hand_over, out_shape=made_shape, in_specs=[anywhere] * 2,...  1.06 us

profile of v3, /device:TPU:12, one launch (start us, length us, event | category | flops | bytes accessed | tf_op | source)
XLA Modules:
  0.0 52.2 jit_solution(12436700063400320272)
XLA Ops:
  0.6 48.5 %shard_map.86 = (f32[1024,128]{1,0:T(8,128)}, f32[640,128]{1,0:T(8,128)}) custom-call(bf16[4,2,640,1024]{3,2,1,0:T(8,128)(2,1)} %bitcast.2, bf16[640,128]{1,0:T(8,128)(2,1)} %y_hbm.1, f32[1024,128]{1,0:T(8,128)} %coef_hbm.1, f32[1,128]{1,0:T(1,128)} %bitcast.3, bf16[1024,128]{1,0:T(8,128)(2,1)} %noise_hbm.1, bf16[1024,512]{1,0:T(8,128)(2,1)} %d_hbm.1, ...), custom_call_target="tpu_custom_call" | custom-call | tf_op jit(solution)/shard_map/pallas_call | solution.py:475
  49.1 0.0 copy-start
  49.1 1.0 %copy-done = f32[1024,128]{1,0:T(8,128)S(1)} copy-done((f32[1024,128]{1,0:T(8,128)S(1)}, f32[1024,128]{1,0:T(8,128)}, u32[]{:S(2)}) %copy-start) | copy-done | bytes 524312
  50.1 0.0 copy-start.1
  50.1 1.0 %copy-done.1 = f32[640,128]{1,0:T(8,128)S(1)} copy-done((f32[640,128]{1,0:T(8,128)S(1)}, f32[640,128]{1,0:T(8,128)}, u32[]{:S(2)}) %copy-start.1) | copy-done | bytes 327704
  51.1 1.1 %shard_map.87 = (f32[1024,128]{1,0:T(8,128)}, f32[640,128]{1,0:T(8,128)}) custom-call(f32[1024,128]{1,0:T(8,128)S(1)} %copy-done, f32[640,128]{1,0:T(8,128)S(1)} %copy-done.1), custom_call_target="tpu_custom_call" | custom-call | tf_op jit(solution)/shard_map/pallas_call | solution.py:495
Async XLA Ops:
  49.1 1.0 %copy-start = (f32[1024,128]{1,0:T(8,128)S(1)}, f32[1024,128]{1,0:T(8,128)}, u32[]{:S(2)}) copy-start(f32[1024,128]{1,0:T(8,128)} %get-tuple-element.4.a_in) | copy-start | bytes 1572868
  50.1 1.0 %copy-start.1 = (f32[640,128]{1,0:T(8,128)S(1)}, f32[640,128]{1,0:T(8,128)}, u32[]{:S(2)}) copy-start(f32[640,128]{1,0:T(8,128)} %get-tuple-element.5.b_in) | copy-start | bytes 983044
